TPU v7x, 256 devices: a whole 4x4x8 slice. The times are simulated.
256 devices in a mesh: team: 2 (over y_hi), gx: 8 (over x, core), gy: 16 (over z, y_lo).
Axes of the slice: x: 4, y: 4 (y_hi: 2, y_lo: 2; y = y_hi * 2 + y_lo), z: 8, core: 2. Of those that a mesh axis runs over, the one named last changes fastest.
Arguments:
- state: float32 [2, 256, 256, 128], P('team', 'gx', 'gy'), may hold values from -6 to 6
- coef: float32 [2, 256, 256, 128], P('team', 'gx', 'gy'), may hold values from 0.5 to 2
- mask: int32 [256, 256, 16], P('gx', 'gy'), may hold values 0 or 1
- src_brick: int32 [8, 16], replicated, may hold values from 0 to 16383
- power: float32 [8, 16], replicated, may hold values from 1 to 4
Outputs:
- final_state: float32 [2, 256, 256, 128], P('team', 'gx', 'gy')
All inputs are finite; a program needn't handle non-finite values. No bound on the sum of `mask` on one device may be relied on, other than what follows from the above.
Results may differ from a plain program's by a relative error of at most 0.00007.
Values sent between devices are 32-bit elements; how exact they have to be, the bound alone decides.
A program may use at most 64 MiB of HBM per device.

v0:
```python
import functools

import jax
import jax.numpy as jnp
from jax import lax
from jax.experimental import pallas as pl
from jax.experimental.pallas import tpu as pltpu
from jax.sharding import PartitionSpec as P

MESH = pl.DeviceIdType.MESH
BRICK = 8
MACRO = 2
SUBS = 4
NSRC = 16
H = 4
BX, BY, NZ = 32, 16, 128
PR = BY + 2 * H
NP = BX + 2 * H
BASE = 32
ROWS = BASE + NP * PR + 32
DIRS = ((-1, 0), (1, 0), (0, -1), (0, 1), (-1, -1), (-1, 1), (1, -1), (1, 1))
OPP = tuple(DIRS.index((-dx, -dy)) for dx, dy in DIRS)
OWN0, BASE0, PART0, OWN1, PART1 = range(5)


def plane(xp):
    return pl.multiple_of(BASE + PR * xp, 8)


def z_next(value, last):
    return jnp.where(last, 0.0, pltpu.roll(value, NZ - 1, 1))


def z_prev(value, first):
    return jnp.where(first, 0.0, pltpu.roll(value, 1, 1))


def lane_ends(rows):
    lane = lax.broadcasted_iota(jnp.int32, (rows, NZ), 1)
    return lane == 0, lane == NZ - 1


def kernel(
    state, coef, mask, bricks, powers, out,
    fu, fb, fl, fk, fq, fa, ff, fm, src, newb, ypack, pbody, xland, yland, cland,
    body_send, body_recv, send, recv,
):
    team, gx, gy = lax.axis_index("team"), lax.axis_index("gx"), lax.axis_index("gy")
    ngx, ngy = lax.axis_size("gx"), lax.axis_size("gy")
    partner = (1 - team, gx, gy)

    def exists(d):
        dx, dy = DIRS[d]
        ok = None
        for delta, pos, size in ((dx, gx, ngx), (dy, gy, ngy)):
            if delta:
                this = pos > 0 if delta < 0 else pos < size - 1
                ok = this if ok is None else jnp.logical_and(ok, this)
        return ok

    def near(d):
        return (team, gx + DIRS[d][0], gy + DIRS[d][1])

    barrier = pltpu.get_barrier_semaphore()
    pl.semaphore_signal(barrier, inc=1, device_id=partner, device_id_type=MESH)
    count = jnp.int32(1)
    for d in range(8):
        @pl.when(exists(d))
        def _():
            pl.semaphore_signal(barrier, inc=1, device_id=near(d), device_id_type=MESH)
        count = count + exists(d).astype(jnp.int32)
    pl.semaphore_wait(barrier, count)

    def body_copy(source, m):
        return pltpu.make_async_remote_copy(
            src_ref=source, dst_ref=pbody.at[m], send_sem=body_send.at[m],
            recv_sem=body_recv.at[m], device_id=partner, device_id_type=MESH,
        )

    def strip(ref_body, kind, d):
        dx, dy = DIRS[d]
        o = OPP[d]
        if dy == 0:
            source = ref_body.at[pl.ds(0 if dx < 0 else BX - H, H)]
            target = xland.at[kind, o]
        elif dx == 0:
            source = ypack.at[kind, d - 2]
            target = yland.at[kind, o - 2]
        else:
            source = ypack.at[kind, 0 if dy < 0 else 1, pl.ds(0 if dx < 0 else (BX - H) * H, H * H)]
            target = cland.at[kind, o - 4]
        return pltpu.make_async_remote_copy(
            src_ref=source, dst_ref=target, send_sem=send.at[kind, d],
            recv_sem=recv.at[kind, o], device_id=near(d), device_id_type=MESH,
        )

    def pack(ref_body, kind):
        @pl.loop(0, BX // 8)
        def _(i):
            for j in range(8):
                x = i * 8 + j
                ypack[kind, 0, pl.ds(pl.multiple_of(i * 32, 32) + 4 * j, H), :] = ref_body[x, 0:H, :]
                ypack[kind, 1, pl.ds(pl.multiple_of(i * 32, 32) + 4 * j, H), :] = ref_body[x, BY - H:BY, :]

    def start_strips(ref_body, kind):
        for d in range(8):
            @pl.when(exists(d))
            def _():
                strip(ref_body, kind, d).start()

    def wait_strips(ref_body, kind):
        for d in range(8):
            @pl.when(exists(d))
            def _():
                recv_wait(kind, d)

    def recv_wait(kind, d):
        dx, dy = DIRS[d]
        if dy == 0:
            ref = xland.at[kind, d]
        elif dx == 0:
            ref = yland.at[kind, d - 2]
        else:
            ref = cland.at[kind, d - 4]
        pltpu.make_async_remote_copy(
            src_ref=ref, dst_ref=ref, send_sem=send.at[kind, d], recv_sem=recv.at[kind, d],
            device_id=near(d), device_id_type=MESH,
        ).wait_recv()

    def wait_sent(ref_body, kind):
        for d in range(8):
            @pl.when(exists(d))
            def _():
                strip(ref_body, kind, d).wait_send()

    def unpack_body(ref_body, flat):
        @pl.loop(0, BX // 4)
        def _(i):
            for j in range(4):
                flat[pl.ds(plane(i * 4 + j + H) + H, BY), :] = ref_body[i * 4 + j]

    def unpack_strips(kind, flat):
        for d in range(8):
            dx, dy = DIRS[d]

            @pl.when(exists(d))
            def _():
                row = 0 if dy < 0 else PR - H
                first = 0 if dx < 0 else NP - H
                if dy == 0:
                    for j in range(H):
                        flat[pl.ds(BASE + PR * (first + j) + H, BY), :] = xland[kind, d, j]
                elif dx == 0:
                    @pl.loop(0, BX // 8)
                    def _(i):
                        for j in range(8):
                            flat[pl.ds(plane(i * 8 + j + H) + row, H), :] = yland[
                                kind, d - 2, pl.ds(pl.multiple_of(i * 32, 32) + 4 * j, H), :
                            ]
                else:
                    for j in range(H):
                        flat[pl.ds(BASE + PR * (first + j) + row, H), :] = cland[
                            kind, d - 4, pl.ds(4 * j, H), :
                        ]

    own = state.at[0]
    body_copy(own, 0).start()
    pack(own, OWN0)
    start_strips(own, OWN0)

    segment = lax.broadcasted_iota(jnp.int32, (NZ // BRICK, NZ), 0)
    spread = (lax.broadcasted_iota(jnp.int32, (NZ // BRICK, NZ), 1) // BRICK == segment).astype(jnp.float32)

    @pl.loop(0, BX // 8)
    def _(i):
        flags = (mask[pl.ds(i * 8, 8)] == 1).astype(jnp.float32).reshape(8 * BY, NZ // BRICK)
        lit = jnp.dot(flags, spread, preferred_element_type=jnp.float32)
        active = jnp.where(lit > 0.5, 1.0, 0.05)
        newb[0, pl.ds(i * 8, 8)] = coef[0, pl.ds(i * 8, 8)] * active.reshape(8, BY, NZ)

    pack(newb.at[0], BASE0)
    start_strips(newb.at[0], BASE0)

    zeros = jnp.zeros((64, NZ), jnp.float32)

    @pl.loop(0, ROWS // 64)
    def _(i):
        at = pl.ds(pl.multiple_of(i * 64, 64), 64)
        fu[0, at, :] = zeros
        fu[1, at, :] = zeros
        fb[at, :] = zeros
        fl[at, :] = zeros
        fk[at, :] = zeros
        fq[at, :] = zeros
        fm[at, :] = zeros

    unpack_body(own, fu.at[0])
    unpack_body(newb.at[0], fb)

    row = lax.broadcasted_iota(jnp.int32, (PR, NZ), 0)
    low = jnp.where(gy == 0, H, 0)
    high = jnp.where(gy == ngy - 1, PR - H, PR)
    factor = jnp.where(team == 0, 0.025, 0.8)
    inside = jnp.where(jnp.logical_and(row >= low, row < high), factor, 0.0)

    @pl.loop(jnp.where(gx == 0, H, 0), jnp.where(gx == ngx - 1, NP - H, NP))
    def _(xp):
        fm[pl.ds(plane(xp), PR), :] = inside

    nbz = NZ // BRICK
    nby = ngy * (BY // BRICK)

    @pl.when(team == 0)
    def _():
        lane_brick = lax.broadcasted_iota(jnp.int32, (PR, NZ), 1) // BRICK
        row_brick = gy * (BY // BRICK) + (row + BRICK - H) // BRICK - 1
        first_x = gx * (BX // BRICK) - 1

        @pl.loop(0, MACRO * SUBS)
        def _(g):
            acc = [jnp.zeros((PR, NZ), jnp.float32) for _ in range(BX // BRICK + 2)]
            for i in range(NSRC):
                b = bricks[g, i]
                p = 2.0 * powers[g, i]
                here = jnp.where(
                    jnp.logical_and(lane_brick == b % nbz, row_brick == (b // nbz) % nby), p, 0.0
                )
                bx = b // (nbz * nby) - first_x
                acc = [a + jnp.where(bx == j, here, 0.0) for j, a in enumerate(acc)]
            for j, a in enumerate(acc):
                src[g, j] = a

    def thermal_prepare():
        _, last = lane_ends(2 * PR)

        @pl.loop(0, NP // 2)
        def _(i):
            at = pl.ds(plane(2 * i), 2 * PR)
            w = fl[at, :]
            slope = z_next(w, last) - w
            fa[at, :] = slope * slope

    def solid_prepare():
        first, last = lane_ends(2 * PR)

        @pl.loop(0, NP // 2)
        def _(i):
            at = pl.ds(plane(2 * i), 2 * PR)
            w = fl[at, :]
            fa[at, :] = 2.0 + 0.5 * w * w
            ff[at, :] = 6.0 * (z_next(w, last) - z_prev(w, first))

    def thermal_step(index, s, cur, nxt, final):
        r = H - 1 - s
        first, last = lane_ends(2 * PR)

        @pl.loop(0, (BX + 2 * r + 2) // 2)
        def _(i):
            at = pl.ds(plane(2 * i + H - r - 1), 2 * PR)
            t = fu[cur, at, :]
            k = fb[at, :] * (1.0 + 0.5 * jnp.tanh(t))
            fk[at, :] = k
            fq[at, :] = k * t

        def update(at0, rows, first, last, heating):
            def faces(load, mid):
                return (
                    (load(-PR) + load(PR)) + (load(-1) + load(1))
                    + (z_next(mid, last) + z_prev(mid, first))
                )
            lu = lambda o: fu[cur, pl.ds(at0 + o, rows), :]
            lk = lambda o: fk[pl.ds(at0 + o, rows), :]
            lq = lambda o: fq[pl.ds(at0 + o, rows), :]
            t, k, q = lu(0), lk(0), lq(0)
            flow = k * faces(lu, t) + faces(lq, q) - t * (6.0 * k + faces(lk, k))
            return t + fm[pl.ds(at0, rows), :] * (flow + heating + fa[pl.ds(at0, rows), :])

        def brick_of(xp):
            return (xp + BRICK - H) // BRICK

        if not final:
            @pl.loop(0, (BX + 2 * r) // 2)
            def _(i):
                xp = 2 * i + H - r
                heating = jnp.concatenate([src[index, brick_of(xp)], src[index, brick_of(xp + 1)]], axis=0)
                fu[nxt, pl.ds(plane(xp), 2 * PR), :] = update(plane(xp), 2 * PR, first, last, heating)
        else:
            f1, l1 = lane_ends(BY)

            @pl.loop(0, BX // 2)
            def _(i):
                for j in range(2):
                    xp = 2 * i + j + H
                    heating = src[index, brick_of(xp), H:H + BY]
                    final[xp - H] = update(plane(xp) + H, BY, f1, l1, heating)

    def solid_step(s, cur, nxt, final):
        r = H - 1 - s
        first, last = lane_ends(2 * PR)

        @pl.loop(0, (BX + 2 * r + 2) // 2)
        def _(i):
            at = pl.ds(plane(2 * i + H - r - 1), 2 * PR)
            u = fu[cur, at, :]
            slope = z_next(u, last) - u
            k = 2.0 * fb[at, :] / (fa[at, :] + slope * slope)
            fk[at, :] = k
            fq[at, :] = k * u

        def update(at0, rows, first, last):
            def solid(load):
                p = load(-PR) + load(PR)
                q = load(-1) + load(1)
                e = (load(-PR - 1) + load(-PR + 1)) + (load(PR - 1) + load(PR + 1))
                h = p + q + 0.5 * e
                return e + z_next(h, last) + z_prev(h, first)
            lu = lambda o: fu[cur, pl.ds(at0 + o, rows), :]
            lk = lambda o: fk[pl.ds(at0 + o, rows), :]
            lq = lambda o: fq[pl.ds(at0 + o, rows), :]
            u, k = lu(0), lk(0)
            top = ff[pl.ds(at0, rows), :] + k * solid(lu) + solid(lq)
            bottom = 16.0 * k + solid(lk) + 6.0
            return 0.2 * u + fm[pl.ds(at0, rows), :] * (top / bottom)

        if not final:
            @pl.loop(0, (BX + 2 * r) // 2)
            def _(i):
                xp = 2 * i + H - r
                fu[nxt, pl.ds(plane(xp), 2 * PR), :] = update(plane(xp), 2 * PR, first, last)
        else:
            f1, l1 = lane_ends(BY)

            @pl.loop(0, BX // 2)
            def _(i):
                for j in range(2):
                    xp = 2 * i + j + H
                    final[xp - H] = update(plane(xp) + H, BY, f1, l1)

    def macro_step(m, final):
        @pl.when(team == 0)
        def _():
            thermal_prepare()
            for s in range(SUBS):
                thermal_step(m * SUBS + s, s, s % 2, 1 - s % 2, final if s == SUBS - 1 else None)

        @pl.when(team == 1)
        def _():
            solid_prepare()
            for s in range(SUBS):
                solid_step(s, s % 2, 1 - s % 2, final if s == SUBS - 1 else None)

    def forward(m, kind):
        body_copy(pbody.at[m], m).wait_recv()
        pack(pbody.at[m], kind)
        start_strips(pbody.at[m], kind)
        unpack_body(pbody.at[m], fl)

    forward(0, PART0)
    wait_strips(own, OWN0)
    unpack_strips(OWN0, fu.at[0])
    wait_strips(newb.at[0], BASE0)
    unpack_strips(BASE0, fb)
    wait_strips(own, PART0)
    unpack_strips(PART0, fl)
    mid = newb.at[1]
    macro_step(0, mid)

    body_copy(mid, 1).start()
    pack(mid, OWN1)
    start_strips(mid, OWN1)
    unpack_body(mid, fu.at[0])
    wait_strips(mid, OWN1)
    unpack_strips(OWN1, fu.at[0])
    forward(1, PART1)
    wait_strips(mid, PART1)
    unpack_strips(PART1, fl)
    macro_step(1, out.at[0])

    body_copy(own, 0).wait_send()
    body_copy(mid, 1).wait_send()
    wait_sent(own, OWN0)
    wait_sent(newb.at[0], BASE0)
    wait_sent(pbody.at[0], PART0)
    wait_sent(mid, OWN1)
    wait_sent(pbody.at[1], PART1)


def local(state, coef, mask, src_brick, power):
    vmem = pl.BlockSpec(memory_space=pltpu.VMEM)
    smem = pl.BlockSpec(memory_space=pltpu.SMEM)
    flat = pltpu.VMEM((ROWS, NZ), jnp.float32)
    return pl.pallas_call(
        kernel,
        name="fields",
        out_shape=jax.ShapeDtypeStruct((1, BX, BY, NZ), jnp.float32),
        in_specs=[vmem, vmem, vmem, smem, smem],
        out_specs=vmem,
        scratch_shapes=[
            pltpu.VMEM((2, ROWS, NZ), jnp.float32),
            flat, flat, flat, flat, flat, flat, flat,
            pltpu.VMEM((MACRO * SUBS, BX // BRICK + 2, PR, NZ), jnp.float32),
            pltpu.VMEM((2, BX, BY, NZ), jnp.float32),
            pltpu.VMEM((5, 2, BX * H, NZ), jnp.float32),
            pltpu.VMEM((2, BX, BY, NZ), jnp.float32),
            pltpu.VMEM((5, 2, H, BY, NZ), jnp.float32),
            pltpu.VMEM((5, 2, BX * H, NZ), jnp.float32),
            pltpu.VMEM((5, 4, H * H, NZ), jnp.float32),
            pltpu.SemaphoreType.DMA((2,)),
            pltpu.SemaphoreType.DMA((2,)),
            pltpu.SemaphoreType.DMA((5, 8)),
            pltpu.SemaphoreType.DMA((5, 8)),
        ],
        compiler_params=pltpu.CompilerParams(
            collective_id=0, has_side_effects=True, vmem_limit_bytes=40 * 2**20
        ),
    )(state, coef, mask, src_brick, power)


def solution(mesh):
    placed = (P("team", "gx", "gy", None), P("team", "gx", "gy", None), P("gx", "gy", None), P(), P())
    return jax.shard_map(
        local, mesh=mesh, in_specs=placed, out_specs=P("team", "gx", "gy", None), check_vma=False
    )
```

profile of v0, /device:TPU:57, one launch (start us, length us, event | category | flops | bytes accessed | tf_op | source)
XLA Modules:
  0.0 73.5 jit_solution(9086174272277822845)
XLA Ops:
  0.0 0.0 copy-start.3
  0.0 0.0 copy-start.2
  0.0 0.0 copy-start
  0.0 1.1 %copy.6.mask = s32[32,16,16]{2,1,0:T(8,128)S(1)} copy(s32[32,16,16]{0,2,1:T(8,128)} %param.7) | data formatting | bytes 65536 | tf_op args[2]
  1.1 0.0 copy-done.3
  1.1 0.0 copy-done.2
  1.1 0.0 copy-done
  1.2 0.0 copy-start.1
  1.2 0.9 %copy-done.1 = f32[1,32,16,128]{3,2,1,0:T(8,128)S(1)} copy-done((f32[1,32,16,128]{3,2,1,0:T(8,128)S(1)}, f32[1,32,16,128]{3,2,1,0:T(8,128)}, u32[]{:S(2)}) %copy-start.1) | copy-done | bytes 262168
  2.1 70.7 %fields.1 = f32[1,32,16,128]{3,2,1,0:T(8,128)S(1)} custom-call(f32[1,32,16,128]{3,2,1,0:T(8,128)S(1)} %copy-done, f32[1,32,16,128]{3,2,1,0:T(8,128)S(1)} %copy-done.1, s32[32,16,16]{2,1,0:T(8,128)S(1)} %copy.6.mask, s32[8,16]{1,0:T(8,128)S(1)} %copy-done.2, f32[8,16]{1,0:T(8,128)S(1)} %copy-done.3), custom_call_target="tpu_custom_call" | custom-call | tf_op jit(solution)/shard_map/fields/pallas_call | solution.py:392
  72.8 0.7 copy.8
Async XLA Ops:
  0.0 1.1 %copy-start.3 = (f32[8,16]{1,0:T(8,128)S(1)}, f32[8,16]{1,0:T(8,128)}, u32[]{:S(2)}) copy-start(f32[8,16]{1,0:T(8,128)} %powers.1) | copy-start | bytes 1540
  0.0 1.1 %copy-start.2 = (s32[8,16]{1,0:T(8,128)S(1)}, s32[8,16]{1,0:T(8,128)}, u32[]{:S(2)}) copy-start(s32[8,16]{1,0:T(8,128)} %bricks.1) | copy-start | bytes 1540
  0.0 1.1 %copy-start = (f32[1,32,16,128]{3,2,1,0:T(8,128)S(1)}, f32[1,32,16,128]{3,2,1,0:T(8,128)}, u32[]{:S(2)}) copy-start(f32[1,32,16,128]{3,2,1,0:T(8,128)} %state.1) | copy-start | bytes 786436
  1.2 1.0 %copy-start.1 = (f32[1,32,16,128]{3,2,1,0:T(8,128)S(1)}, f32[1,32,16,128]{3,2,1,0:T(8,128)}, u32[]{:S(2)}) copy-start(f32[1,32,16,128]{3,2,1,0:T(8,128)} %coef.1) | copy-start | bytes 786436
where the time goes:
time: 74.7 us; the launch traced here: 73.5 us
  Pallas kernels  70.7 us (95%)
  local copies, waits for them, and re-layouts  2.77 us (4%)
    pallas_call x1, Pallas kernels, local(): pl.pallas_call(kernel, name='fields', out_shape=jax.ShapeDtypeStruct((1,...  70.7 us
    unnamed x10, local copies, waits for them, and re-layouts  2.77 us

commit v1 on v0

v1 whole, which is shorter than its diff:
```python
import jax
import jax.numpy as jnp
from jax import lax
from jax.experimental import pallas as pl
from jax.experimental.pallas import tpu as pltpu
from jax.sharding import PartitionSpec as P

MESH = pl.DeviceIdType.MESH
BRICK = 8
MACRO = 2
SUBS = 4
NSRC = 16
H = 4
BX, BY, NZ = 32, 16, 128
PR = BY + 2 * H
NP = BX + 2 * H
BASE = 32
ROWS = BASE + NP * PR + 32
CHUNK = 192
DIRS = ((-1, 0), (1, 0), (0, -1), (0, 1), (-1, -1), (-1, 1), (1, -1), (1, 1))
OPP = tuple(DIRS.index((-dx, -dy)) for dx, dy in DIRS)
OWN0, BASE0, PART0, OWN1, PART1 = range(5)

PIECES = ((0, H), (BX - H, H), (H, BX - 2 * H))


def row_of(xp):
    return BASE + PR * xp


def z_next(value):
    lane = lax.broadcasted_iota(jnp.int32, value.shape, 1)
    return jnp.where(lane == NZ - 1, 0.0, pltpu.roll(value, NZ - 1, 1))


def z_prev(value):
    lane = lax.broadcasted_iota(jnp.int32, value.shape, 1)
    return jnp.where(lane == 0, 0.0, pltpu.roll(value, 1, 1))


def shift_matrix():
    source = lax.broadcasted_iota(jnp.int32, (NZ, 2 * NZ), 0)
    target = lax.broadcasted_iota(jnp.int32, (NZ, 2 * NZ), 1)
    following = jnp.logical_and(target < NZ, source == target + 1)
    previous = jnp.logical_and(target >= NZ, source == target - NZ - 1)
    once = jnp.logical_or(following, previous).astype(jnp.bfloat16)
    return jnp.concatenate([once, once], axis=0)


def z_both(value, matrix):
    high = value.astype(jnp.bfloat16)
    rest = (value - high.astype(jnp.float32)).astype(jnp.bfloat16)
    both = jnp.dot(jnp.concatenate([high, rest], axis=1), matrix, preferred_element_type=jnp.float32)
    return both[:, :NZ], both[:, NZ:]


def kernel(
    state, coef, mask_in, bricks_in, powers_in, out,
    fu, fb, fl, vz, fa, ff, fm, src, sv, cv, nb, act, pk, pb, xland, yland, cland, mask, bricks, powers,
    local_sem, body_send, body_recv, send, recv,
):
    team, gx, gy = lax.axis_index("team"), lax.axis_index("gx"), lax.axis_index("gy")
    ngx, ngy = lax.axis_size("gx"), lax.axis_size("gy")
    partner = (1 - team, gx, gy)

    state_copy = pltpu.make_async_copy(state.at[0], sv, local_sem.at[0])
    coef_copy = pltpu.make_async_copy(coef.at[0], cv, local_sem.at[1])
    mask_copy = pltpu.make_async_copy(mask_in, mask, local_sem.at[2])
    brick_copy = pltpu.make_async_copy(bricks_in, bricks, local_sem.at[3])
    power_copy = pltpu.make_async_copy(powers_in, powers, local_sem.at[4])
    state_copy.start()
    coef_copy.start()
    mask_copy.start()
    brick_copy.start()
    power_copy.start()

    def exists(d):
        dx, dy = DIRS[d]
        ok = None
        for delta, pos, size in ((dx, gx, ngx), (dy, gy, ngy)):
            if delta:
                this = pos > 0 if delta < 0 else pos < size - 1
                ok = this if ok is None else jnp.logical_and(ok, this)
        return ok

    def near(d, crossed=False):
        return (1 - team if crossed else team, gx + DIRS[d][0], gy + DIRS[d][1])

    barrier = pltpu.get_barrier_semaphore()
    pl.semaphore_signal(barrier, inc=1, device_id=partner, device_id_type=MESH)
    count = jnp.int32(1)
    for d in range(8):
        @pl.when(exists(d))
        def _():
            pl.semaphore_signal(barrier, inc=1, device_id=near(d), device_id_type=MESH)
            if d >= 2:
                pl.semaphore_signal(barrier, inc=1, device_id=near(d, True), device_id_type=MESH)
        count = count + (2 if d >= 2 else 1) * exists(d).astype(jnp.int32)

    def body_copy(source, m, piece):
        first, planes = PIECES[piece]
        return pltpu.make_async_remote_copy(
            src_ref=source.at[pl.ds(first, planes)], dst_ref=pb.at[m, pl.ds(first, planes)],
            send_sem=body_send.at[m, piece], recv_sem=body_recv.at[m, piece],
            device_id=partner, device_id_type=MESH,
        )

    strips = {
        OWN0: (sv, pk.at[0], False),
        BASE0: (cv, pk.at[2], False),
        PART0: (pb.at[0], pk.at[0], True),
        OWN1: (nb, pk.at[1], False),
        PART1: (pb.at[1], pk.at[1], True),
    }
    ALONG_Y = (2, 3, 4, 5, 6, 7)

    def strip(kind, d):
        block, packed, crossed = strips[kind]
        dx, dy = DIRS[d]
        o = OPP[d]
        if dy == 0:
            source = block.at[pl.ds(0 if dx < 0 else BX - H, H)]
            target = xland.at[kind, o]
        elif dx == 0:
            source = packed.at[d - 2]
            target = yland.at[kind, o - 2]
        else:
            source = packed.at[0 if dy < 0 else 1, pl.ds(0 if dx < 0 else (BX - H) * H, H * H)]
            target = cland.at[kind, o - 4]
        return pltpu.make_async_remote_copy(
            src_ref=source, dst_ref=target, send_sem=send.at[kind, d],
            recv_sem=recv.at[kind, o], device_id=near(d, crossed and d >= 2), device_id_type=MESH,
        )

    def start_strips(kind, ways):
        for d in ways:
            @pl.when(exists(d))
            def _():
                strip(kind, d).start()

    def landing(kind, d):
        return xland.at[kind, d] if d < 2 else yland.at[kind, d - 2] if d < 4 else cland.at[kind, d - 4]

    def receive_strips(kind, flat):
        for d in (0, 1) + ALONG_Y:
            dx, dy = DIRS[d]

            @pl.when(exists(d))
            def _():
                ref = landing(kind, d)
                pltpu.make_async_remote_copy(
                    src_ref=ref, dst_ref=ref, send_sem=send.at[kind, d], recv_sem=recv.at[kind, d],
                    device_id=near(d), device_id_type=MESH,
                ).wait_recv()
                row = 0 if dy < 0 else PR - H
                first = 0 if dx < 0 else NP - H
                if dy == 0:
                    for j in range(H):
                        flat[pl.ds(row_of(first + j) + H, BY), :] = xland[kind, d, j]
                elif dx == 0:
                    for x in range(BX):
                        flat[pl.ds(row_of(x + H) + row, H), :] = yland[kind, d - 2, pl.ds(H * x, H), :]
                else:
                    for j in range(H):
                        flat[pl.ds(row_of(first + j) + row, H), :] = cland[kind, d - 4, pl.ds(H * j, H), :]

    def wait_sent(kind):
        for d in range(8):
            @pl.when(exists(d))
            def _():
                strip(kind, d).wait_send()

    def pack(slot, block):
        for x in range(BX):
            pk[slot, 0, pl.ds(H * x, H), :] = block[x, 0:H, :]
            pk[slot, 1, pl.ds(H * x, H), :] = block[x, BY - H:BY, :]

    def send_block(block, slot, m, own, other):
        body_copy(block, m, 0).start()
        body_copy(block, m, 1).start()
        pack(slot, block)
        start_strips(other, ALONG_Y)
        start_strips(own, ALONG_Y + (0, 1))
        body_copy(block, m, 2).start()

    def forward(m, kind):
        for side in range(2):
            body_copy(nb, m, side).wait_recv()
            start_strips(kind, (side,))

    def unpack_partner(m):
        body_copy(nb, m, 2).wait_recv()
        for x in range(BX):
            fl[pl.ds(row_of(x + H) + H, BY), :] = pb[m, x]

    state_copy.wait()
    pl.semaphore_wait(barrier, count)
    send_block(sv, 0, 0, OWN0, PART0)

    segment = lax.broadcasted_iota(jnp.int32, (NZ // BRICK, NZ), 0)
    spread = (lax.broadcasted_iota(jnp.int32, (NZ // BRICK, NZ), 1) // BRICK == segment).astype(jnp.float32)
    unit = jnp.where(team == 0, 1.0, 2.0)
    mask_copy.wait()
    for y in range(BY):
        lit = lax.dot_general(
            (mask[y] == 1).astype(jnp.float32), spread, (((0,), (0,)), ((), ())),
            preferred_element_type=jnp.float32,
        )
        act[pl.ds(y * BX, BX), :] = jnp.where(lit > 0.5, unit, 0.05 * unit)
    coef_copy.wait()
    for x in range(BX):
        cv[x] = cv[x] * act[pl.ds(x, BY, stride=BX), :]
    pack(2, cv)
    start_strips(BASE0, ALONG_Y + (0, 1))

    zeros = jnp.zeros((64, NZ), jnp.float32)

    @pl.loop(0, ROWS // 64)
    def _(i):
        at = pl.ds(pl.multiple_of(i * 64, 64), 64)
        fu[0, at, :] = zeros
        fu[1, at, :] = zeros
        fb[at, :] = zeros
        fl[at, :] = zeros
        fm[at, :] = zeros

    for x in range(BX):
        at = pl.ds(row_of(x + H) + H, BY)
        fu[0, at, :] = sv[x]
        fb[at, :] = cv[x]

    row = lax.broadcasted_iota(jnp.int32, (PR, NZ), 0)
    low = jnp.where(gy == 0, H, 0)
    high = jnp.where(gy == ngy - 1, PR - H, PR)
    factor = jnp.where(team == 0, 0.025, 0.8)
    inside = jnp.where(jnp.logical_and(row >= low, row < high), factor, 0.0)

    @pl.loop(jnp.where(gx == 0, H, 0), jnp.where(gx == ngx - 1, NP - H, NP))
    def _(xp):
        fm[pl.ds(pl.multiple_of(row_of(xp), 8), PR), :] = inside

    forward(0, PART0)
    brick_copy.wait()
    power_copy.wait()

    nbz = NZ // BRICK
    nby = ngy * (BY // BRICK)

    @pl.when(team == 0)
    def _():
        lane_brick = lax.broadcasted_iota(jnp.int32, (PR, NZ), 1) // BRICK
        row_brick = gy * (BY // BRICK) + (row + BRICK - H) // BRICK - 1
        first_x = gx * (BX // BRICK) - 1

        @pl.loop(0, MACRO * SUBS)
        def _(g):
            acc = [jnp.zeros((PR, NZ), jnp.float32) for _ in range(BX // BRICK + 2)]
            for i in range(NSRC):
                b = bricks[g, i]
                p = 2.0 * powers[g, i]
                here = jnp.where(
                    jnp.logical_and(lane_brick == b % nbz, row_brick == (b // nbz) % nby), p, 0.0
                )
                bx = b // (nbz * nby) - first_x
                acc = [a + jnp.where(bx == j, here, 0.0) for j, a in enumerate(acc)]
            for j, a in enumerate(acc):
                src[g, j] = a

    unpack_partner(0)
    receive_strips(OWN0, fu.at[0])
    receive_strips(BASE0, fb)
    receive_strips(PART0, fl)

    matrix = shift_matrix()

    def thermal_prepare():
        for i in range(NP * PR // CHUNK):
            at = pl.ds(BASE + CHUNK * i, CHUNK)
            w = fl[at, :]
            slope = z_next(w) - w
            fa[at, :] = slope * slope

    def solid_prepare():
        for i in range(NP * PR // CHUNK):
            at = pl.ds(BASE + CHUNK * i, CHUNK)
            w = fl[at, :]
            fa[at, :] = 2.0 + 0.5 * w * w
            ff[at, :] = 6.0 * (z_next(w) - z_prev(w))

    def lateral(parts, finish):
        for c in range(PR // 8):
            window = [parts(x, c) for x in (0, 1)]
            for x in range(1, NP - 1):
                window.append(parts(x + 1, c))
                below, here, above = window
                finish(x, c, [lo[0] + hi[0] + me[1] for lo, me, hi in zip(below, here, above)])
                window.pop(0)

    def thermal_step(g, cur, nxt):
        for i in range(NP * PR // CHUNK):
            at = pl.ds(BASE + CHUNK * i, CHUNK)
            t = fu[cur, at, :]
            tp, tn = z_next(t), z_prev(t)
            k = fb[at, :] * (1.0 + 0.5 * jnp.tanh(t))
            kp, kn = z_both(k, matrix)
            vz[0, at, :] = k
            vz[1, at, :] = k * t
            vz[2, at, :] = tp + tn
            vz[3, at, :] = kp + kn
            vz[4, at, :] = kp * tp + kn * tn

        def parts(x, c):
            at = row_of(x) + 8 * c
            found = []
            for load, z in ((lambda r: fu[cur, pl.ds(r, 8), :], 2), (lambda r: vz[0, pl.ds(r, 8), :], 3),
                            (lambda r: vz[1, pl.ds(r, 8), :], 4)):
                found.append((load(at), load(at - 1) + load(at + 1) + vz[z, pl.ds(at, 8), :]))
            return found

        def finish(x, c, sums):
            at = pl.ds(row_of(x) + 8 * c, 8)
            t, k = fu[cur, at, :], vz[0, at, :]
            flow = k * sums[0] + sums[2] - t * (6.0 * k + sums[1])
            heating = src[g, (x + BRICK - H) // BRICK, pl.ds(8 * c, 8), :]
            fu[nxt, at, :] = t + fm[at, :] * (flow + heating + fa[at, :])

        lateral(parts, finish)

    def solid_step(cur, nxt):
        for i in range(NP * PR // CHUNK):
            at = pl.ds(BASE + CHUNK * i, CHUNK)
            u = fu[cur, at, :]
            up, un = z_next(u), z_prev(u)
            slope = up - u
            k = fb[at, :] / (fa[at, :] + slope * slope)
            kp, kn = z_both(k, matrix)
            for j, (value, both) in enumerate(((u, up + un), (k, kp + kn), (k * u, kp * up + kn * un))):
                vz[2 * j, at, :] = value + 0.5 * both
                vz[2 * j + 1, at, :] = both
            vz[6, at, :] = k

        def parts(x, c):
            at = row_of(x) + 8 * c
            found = []
            for j in range(3):
                whole = lambda r: vz[2 * j, pl.ds(r, 8), :]
                both = lambda r: vz[2 * j + 1, pl.ds(r, 8), :]
                found.append((whole(at - 1) + whole(at + 1) + both(at), both(at - 1) + both(at + 1)))
            return found

        def finish(x, c, sums):
            at = pl.ds(row_of(x) + 8 * c, 8)
            u, k = fu[cur, at, :], vz[6, at, :]
            top = ff[at, :] + k * sums[0] + sums[2]
            bottom = 16.0 * k + sums[1] + 6.0
            fu[nxt, at, :] = 0.2 * u + fm[at, :] * (top / bottom)

        lateral(parts, finish)

    @pl.loop(0, MACRO)
    def _(m):
        @pl.when(team == 0)
        def _():
            thermal_prepare()

            @pl.loop(0, SUBS // 2)
            def _(i):
                thermal_step(m * SUBS + 2 * i, 0, 1)
                thermal_step(m * SUBS + 2 * i + 1, 1, 0)

        @pl.when(team == 1)
        def _():
            solid_prepare()

            @pl.loop(0, SUBS // 2)
            def _(i):
                solid_step(0, 1)
                solid_step(1, 0)

        @pl.when(m == 0)
        def _():
            for x in range(BX):
                nb[x] = fu[0, pl.ds(row_of(x + H) + H, BY), :]
            send_block(nb, 1, 1, OWN1, PART1)
            forward(1, PART1)
            unpack_partner(1)
            receive_strips(OWN1, fu.at[0])
            receive_strips(PART1, fl)

    for x in range(BX):
        out[0, x] = fu[0, pl.ds(row_of(x + H) + H, BY), :]

    for m in range(MACRO):
        for piece in range(3):
            body_copy(nb, m, piece).wait_send()
    for kind in range(5):
        wait_sent(kind)


def local(state, coef, mask, src_brick, power):
    vmem = pl.BlockSpec(memory_space=pltpu.VMEM)
    hbm = pl.BlockSpec(memory_space=pltpu.HBM)
    flat = pltpu.VMEM((ROWS, NZ), jnp.float32)
    block = pltpu.VMEM((BX, BY, NZ), jnp.float32)
    return pl.pallas_call(
        kernel,
        name="fields",
        out_shape=jax.ShapeDtypeStruct((1, BX, BY, NZ), jnp.float32),
        in_specs=[hbm] * 5,
        out_specs=vmem,
        scratch_shapes=[
            pltpu.VMEM((2, ROWS, NZ), jnp.float32),
            flat, flat,
            pltpu.VMEM((7, ROWS, NZ), jnp.float32),
            flat, flat, flat,
            pltpu.VMEM((MACRO * SUBS, BX // BRICK + 2, PR, NZ), jnp.float32),
            block, block, block,
            pltpu.VMEM((BY * BX, NZ), jnp.float32),
            pltpu.VMEM((3, 2, BX * H, NZ), jnp.float32),
            pltpu.VMEM((2, BX, BY, NZ), jnp.float32),
            pltpu.VMEM((5, 2, H, BY, NZ), jnp.float32),
            pltpu.VMEM((5, 2, BX * H, NZ), jnp.float32),
            pltpu.VMEM((5, 4, H * H, NZ), jnp.float32),
            pltpu.VMEM((BY, NZ // BRICK, BX), jnp.int32),
            pltpu.SMEM((MACRO * SUBS, NSRC), jnp.int32),
            pltpu.SMEM((MACRO * SUBS, NSRC), jnp.float32),
            pltpu.SemaphoreType.DMA((5,)),
            pltpu.SemaphoreType.DMA((2, 3)),
            pltpu.SemaphoreType.DMA((2, 3)),
            pltpu.SemaphoreType.DMA((5, 8)),
            pltpu.SemaphoreType.DMA((5, 8)),
        ],
        compiler_params=pltpu.CompilerParams(
            collective_id=0, has_side_effects=True, vmem_limit_bytes=60 * 2**20
        ),
    )(state, coef, jnp.transpose(mask, (1, 2, 0)), src_brick, power)


def solution(mesh):
    placed = (P("team", "gx", "gy", None), P("team", "gx", "gy", None), P("gx", "gy", None), P(), P())
    return jax.shard_map(
        local, mesh=mesh, in_specs=placed, out_specs=P("team", "gx", "gy", None), check_vma=False
    )
```

time: 74.7 us -> 43.3 us (0.58)
  the two profiles are of different devices: /device:TPU:57 before, /device:TPU:100 now
where the time goes in v1:
time: 43.3 us; the launch traced here: 43.1 us
  Pallas kernels  41.5 us (96%)
  local copies, waits for them, and re-layouts  1.67 us (4%)
    pallas_call x1, Pallas kernels, local(): pl.pallas_call(kernel, name='fields', out_shape=jax.ShapeDtypeStruct((1,...  41.5 us
    unnamed x1, local copies, waits for them, and re-layouts  1.67 us

profile of v1, /device:TPU:100, one launch (start us, length us, event | category | flops | bytes accessed | tf_op | source)
XLA Modules:
  0.0 43.1 jit_solution(8275732347559510387)
XLA Ops:
  0.0 41.5 %fields.1 = f32[1,32,16,128]{3,2,1,0:T(8,128)} custom-call(f32[1,32,16,128]{3,2,1,0:T(8,128)} %state.1, f32[1,32,16,128]{3,2,1,0:T(8,128)} %coef.1, s32[16,16,32]{2,1,0:T(8,128)} %bitcast.1, s32[8,16]{1,0:T(8,128)} %bricks_in.1, f32[8,16]{1,0:T(8,128)} %powers_in.1), custom_call_target="tpu_custom_call" | custom-call | tf_op jit(solution)/shard_map/fields/pallas_call | solution.py:405
  41.5 1.7 %copy.7 = f32[1,32,16,128]{3,2,1,0:T(8,128)} copy(f32[1,32,16,128]{3,2,1,0:T(8,128)} %fields.1) | data formatting | bytes 524288

commit v2 on v1

--- a/solution.py
+++ b/solution.py
@@ -18,8 +18,9 @@
 ROWS = BASE + NP * PR + 32
 CHUNK = 192
 DIRS = ((-1, 0), (1, 0), (0, -1), (0, 1), (-1, -1), (-1, 1), (1, -1), (1, 1))
+KINDS = 5
 OPP = tuple(DIRS.index((-dx, -dy)) for dx, dy in DIRS)
-OWN0, BASE0, PART0, OWN1, PART1 = range(5)
+OWN0, BASE0, PART0, OWN1, PART1 = range(KINDS)
 
 PIECES = ((0, H), (BX - H, H), (H, BX - 2 * H))
 
@@ -89,7 +90,7 @@
     barrier = pltpu.get_barrier_semaphore()
     pl.semaphore_signal(barrier, inc=1, device_id=partner, device_id_type=MESH)
     count = jnp.int32(1)
-    for d in range(8):
+    for d in range(4):
         @pl.when(exists(d))
         def _():
             pl.semaphore_signal(barrier, inc=1, device_id=near(d), device_id_type=MESH)
@@ -112,24 +113,27 @@
         OWN1: (nb, pk.at[1], False),
         PART1: (pb.at[1], pk.at[1], True),
     }
-    ALONG_Y = (2, 3, 4, 5, 6, 7)
+    ALONG_X, ALONG_Y = (0, 1), (2, 3)
 
     def strip(kind, d):
         block, packed, crossed = strips[kind]
         dx, dy = DIRS[d]
-        o = OPP[d]
         if dy == 0:
+            o = OPP[d]
             source = block.at[pl.ds(0 if dx < 0 else BX - H, H)]
             target = xland.at[kind, o]
         elif dx == 0:
+            o = OPP[d]
             source = packed.at[d - 2]
             target = yland.at[kind, o - 2]
         else:
-            source = packed.at[0 if dy < 0 else 1, pl.ds(0 if dx < 0 else (BX - H) * H, H * H)]
+            o = DIRS.index((-dx, dy))
+            source = yland.at[kind, 0 if dy < 0 else 1, pl.ds(0 if dx < 0 else (BX - H) * H, H * H)]
             target = cland.at[kind, o - 4]
+        to = near(d, crossed) if dx == 0 else (team, gx + dx, gy)
         return pltpu.make_async_remote_copy(
             src_ref=source, dst_ref=target, send_sem=send.at[kind, d],
-            recv_sem=recv.at[kind, o], device_id=near(d, crossed and d >= 2), device_id_type=MESH,
+            recv_sem=recv.at[kind, o], device_id=to, device_id_type=MESH,
         )
 
     def start_strips(kind, ways):
@@ -141,17 +145,32 @@
     def landing(kind, d):
         return xland.at[kind, d] if d < 2 else yland.at[kind, d - 2] if d < 4 else cland.at[kind, d - 4]
 
-    def receive_strips(kind, flat):
-        for d in (0, 1) + ALONG_Y:
-            dx, dy = DIRS[d]
-
+    def arrived(kind, d):
+        ref = landing(kind, d)
+        pltpu.make_async_remote_copy(
+            src_ref=ref, dst_ref=ref, send_sem=send.at[kind, d], recv_sem=recv.at[kind, d],
+            device_id=near(d % 4), device_id_type=MESH,
+        ).wait_recv()
+
+    def relay(kind):
+        for d in ALONG_Y:
             @pl.when(exists(d))
             def _():
-                ref = landing(kind, d)
-                pltpu.make_async_remote_copy(
-                    src_ref=ref, dst_ref=ref, send_sem=send.at[kind, d], recv_sem=recv.at[kind, d],
-                    device_id=near(d), device_id_type=MESH,
-                ).wait_recv()
+                arrived(kind, d)
+                for corner in range(4, 8):
+                    if DIRS[corner][1] == DIRS[d][1]:
+                        @pl.when(exists(corner))
+                        def _():
+                            strip(kind, corner).start()
+
+    def receive_strips(kind, flat):
+        for d in ALONG_Y + ALONG_X + (4, 5, 6, 7):
+            dx, dy = DIRS[d]
+
+            @pl.when(exists(d))
+            def _():
+                if d not in ALONG_Y:
+                    arrived(kind, d)
                 row = 0 if dy < 0 else PR - H
                 first = 0 if dx < 0 else NP - H
                 if dy == 0:
@@ -180,7 +199,7 @@
         body_copy(block, m, 1).start()
         pack(slot, block)
         start_strips(other, ALONG_Y)
-        start_strips(own, ALONG_Y + (0, 1))
+        start_strips(own, ALONG_Y + ALONG_X)
         body_copy(block, m, 2).start()
 
     def forward(m, kind):
@@ -211,7 +230,7 @@
     for x in range(BX):
         cv[x] = cv[x] * act[pl.ds(x, BY, stride=BX), :]
     pack(2, cv)
-    start_strips(BASE0, ALONG_Y + (0, 1))
+    start_strips(BASE0, ALONG_Y + ALONG_X)
 
     zeros = jnp.zeros((64, NZ), jnp.float32)
 
@@ -223,6 +242,11 @@
         fb[at, :] = zeros
         fl[at, :] = zeros
         fm[at, :] = zeros
+
+    guard = jnp.zeros((8, NZ), jnp.float32)
+    for j in range(7):
+        vz[j, pl.ds(BASE - 8, 8), :] = guard
+        vz[j, pl.ds(row_of(NP), 8), :] = guard
 
     for x in range(BX):
         at = pl.ds(row_of(x + H) + H, BY)
@@ -266,9 +290,12 @@
             for j, a in enumerate(acc):
                 src[g, j] = a
 
-    unpack_partner(0)
+    relay(OWN0)
+    relay(PART0)
+    relay(BASE0)
     receive_strips(OWN0, fu.at[0])
     receive_strips(BASE0, fb)
+    unpack_partner(0)
     receive_strips(PART0, fl)
 
     matrix = shift_matrix()
@@ -288,7 +315,8 @@
             ff[at, :] = 6.0 * (z_next(w) - z_prev(w))
 
     def lateral(parts, finish):
-        for c in range(PR // 8):
+        @pl.loop(0, PR // 8)
+        def _(c):
             window = [parts(x, c) for x in (0, 1)]
             for x in range(1, NP - 1):
                 window.append(parts(x + 1, c))
@@ -310,7 +338,7 @@
             vz[4, at, :] = kp * tp + kn * tn
 
         def parts(x, c):
-            at = row_of(x) + 8 * c
+            at = pl.multiple_of(row_of(x) + 8 * c, 8)
             found = []
             for load, z in ((lambda r: fu[cur, pl.ds(r, 8), :], 2), (lambda r: vz[0, pl.ds(r, 8), :], 3),
                             (lambda r: vz[1, pl.ds(r, 8), :], 4)):
@@ -318,10 +346,10 @@
             return found
 
         def finish(x, c, sums):
-            at = pl.ds(row_of(x) + 8 * c, 8)
+            at = pl.ds(pl.multiple_of(row_of(x) + 8 * c, 8), 8)
             t, k = fu[cur, at, :], vz[0, at, :]
             flow = k * sums[0] + sums[2] - t * (6.0 * k + sums[1])
-            heating = src[g, (x + BRICK - H) // BRICK, pl.ds(8 * c, 8), :]
+            heating = src[g, (x + BRICK - H) // BRICK, pl.ds(pl.multiple_of(8 * c, 8), 8), :]
             fu[nxt, at, :] = t + fm[at, :] * (flow + heating + fa[at, :])
 
         lateral(parts, finish)
@@ -340,7 +368,7 @@
             vz[6, at, :] = k
 
         def parts(x, c):
-            at = row_of(x) + 8 * c
+            at = pl.multiple_of(row_of(x) + 8 * c, 8)
             found = []
             for j in range(3):
                 whole = lambda r: vz[2 * j, pl.ds(r, 8), :]
@@ -349,7 +377,7 @@
             return found
 
         def finish(x, c, sums):
-            at = pl.ds(row_of(x) + 8 * c, 8)
+            at = pl.ds(pl.multiple_of(row_of(x) + 8 * c, 8), 8)
             u, k = fu[cur, at, :], vz[6, at, :]
             top = ff[at, :] + k * sums[0] + sums[2]
             bottom = 16.0 * k + sums[1] + 6.0
@@ -383,8 +411,10 @@
                 nb[x] = fu[0, pl.ds(row_of(x + H) + H, BY), :]
             send_block(nb, 1, 1, OWN1, PART1)
             forward(1, PART1)
+            relay(OWN1)
+            relay(PART1)
+            receive_strips(OWN1, fu.at[0])
             unpack_partner(1)
-            receive_strips(OWN1, fu.at[0])
             receive_strips(PART1, fl)
 
     for x in range(BX):
@@ -393,7 +423,7 @@
     for m in range(MACRO):
         for piece in range(3):
             body_copy(nb, m, piece).wait_send()
-    for kind in range(5):
+    for kind in range(KINDS):
         wait_sent(kind)
 
 
@@ -418,17 +448,17 @@
             pltpu.VMEM((BY * BX, NZ), jnp.float32),
             pltpu.VMEM((3, 2, BX * H, NZ), jnp.float32),
             pltpu.VMEM((2, BX, BY, NZ), jnp.float32),
-            pltpu.VMEM((5, 2, H, BY, NZ), jnp.float32),
-            pltpu.VMEM((5, 2, BX * H, NZ), jnp.float32),
-            pltpu.VMEM((5, 4, H * H, NZ), jnp.float32),
+            pltpu.VMEM((KINDS, 2, H, BY, NZ), jnp.float32),
+            pltpu.VMEM((KINDS, 2, BX * H, NZ), jnp.float32),
+            pltpu.VMEM((KINDS, 4, H * H, NZ), jnp.float32),
             pltpu.VMEM((BY, NZ // BRICK, BX), jnp.int32),
             pltpu.SMEM((MACRO * SUBS, NSRC), jnp.int32),
             pltpu.SMEM((MACRO * SUBS, NSRC), jnp.float32),
             pltpu.SemaphoreType.DMA((5,)),
             pltpu.SemaphoreType.DMA((2, 3)),
             pltpu.SemaphoreType.DMA((2, 3)),
-            pltpu.SemaphoreType.DMA((5, 8)),
-            pltpu.SemaphoreType.DMA((5, 8)),
+            pltpu.SemaphoreType.DMA((KINDS, 8)),
+            pltpu.SemaphoreType.DMA((KINDS, 8)),
         ],
         compiler_params=pltpu.CompilerParams(
             collective_id=0, has_side_effects=True, vmem_limit_bytes=60 * 2**20

time: 43.3 us -> 41 us (0.947)
  the two profiles are of different devices: /device:TPU:100 before, /device:TPU:123 now
where the time goes in v2:
time: 41 us; the launch traced here: 40.9 us
  Pallas kernels  39.2 us (96%)
  local copies, waits for them, and re-layouts  1.67 us (4%)
    pallas_call x1, Pallas kernels, local(): pl.pallas_call(kernel, name='fields', out_shape=jax.ShapeDtypeStruct((1,...  39.2 us
    unnamed x1, local copies, waits for them, and re-layouts  1.67 us

profile of v2, /device:TPU:123, one launch (start us, length us, event | category | flops | bytes accessed | tf_op | source)
XLA Modules:
  0.0 40.9 jit_solution(17556307708889379792)
XLA Ops:
  0.0 39.2 %fields.1 = f32[1,32,16,128]{3,2,1,0:T(8,128)} custom-call(f32[1,32,16,128]{3,2,1,0:T(8,128)} %state.1, f32[1,32,16,128]{3,2,1,0:T(8,128)} %coef.1, s32[16,16,32]{2,1,0:T(8,128)} %bitcast.1, s32[8,16]{1,0:T(8,128)} %bricks_in.1, f32[8,16]{1,0:T(8,128)} %powers_in.1), custom_call_target="tpu_custom_call" | custom-call | tf_op jit(solution)/shard_map/fields/pallas_call | solution.py:435
  39.2 1.7 %copy.7 = f32[1,32,16,128]{3,2,1,0:T(8,128)} copy(f32[1,32,16,128]{3,2,1,0:T(8,128)} %fields.1) | data formatting | bytes 524288

commit v3 on v2

--- a/solution.py
+++ b/solution.py
@@ -200,7 +200,8 @@
         pack(slot, block)
         start_strips(other, ALONG_Y)
         start_strips(own, ALONG_Y + ALONG_X)
-        body_copy(block, m, 2).start()
+        if m:
+            body_copy(block, m, 2).start()
 
     def forward(m, kind):
         for side in range(2):
@@ -231,6 +232,7 @@
         cv[x] = cv[x] * act[pl.ds(x, BY, stride=BX), :]
     pack(2, cv)
     start_strips(BASE0, ALONG_Y + ALONG_X)
+    body_copy(sv, 0, 2).start()
 
     zeros = jnp.zeros((64, NZ), jnp.float32)
 
@@ -266,6 +268,9 @@
     forward(0, PART0)
     brick_copy.wait()
     power_copy.wait()
+
+    relay(OWN0)
+    relay(PART0)
 
     nbz = NZ // BRICK
     nby = ngy * (BY // BRICK)
@@ -290,8 +295,6 @@
             for j, a in enumerate(acc):
                 src[g, j] = a
 
-    relay(OWN0)
-    relay(PART0)
     relay(BASE0)
     receive_strips(OWN0, fu.at[0])
     receive_strips(BASE0, fb)
@@ -314,11 +317,11 @@
             fa[at, :] = 2.0 + 0.5 * w * w
             ff[at, :] = 6.0 * (z_next(w) - z_prev(w))
 
-    def lateral(parts, finish):
+    def lateral(parts, finish, skip):
         @pl.loop(0, PR // 8)
         def _(c):
-            window = [parts(x, c) for x in (0, 1)]
-            for x in range(1, NP - 1):
+            window = [parts(x, c) for x in (skip - 1, skip)]
+            for x in range(skip, NP - skip):
                 window.append(parts(x + 1, c))
                 below, here, above = window
                 finish(x, c, [lo[0] + hi[0] + me[1] for lo, me, hi in zip(below, here, above)])
@@ -352,7 +355,7 @@
             heating = src[g, (x + BRICK - H) // BRICK, pl.ds(pl.multiple_of(8 * c, 8), 8), :]
             fu[nxt, at, :] = t + fm[at, :] * (flow + heating + fa[at, :])
 
-        lateral(parts, finish)
+        lateral(parts, finish, 1 + cur)
 
     def solid_step(cur, nxt):
         for i in range(NP * PR // CHUNK):
@@ -383,7 +386,7 @@
             bottom = 16.0 * k + sums[1] + 6.0
             fu[nxt, at, :] = 0.2 * u + fm[at, :] * (top / bottom)
 
-        lateral(parts, finish)
+        lateral(parts, finish, 1 + cur)
 
     @pl.loop(0, MACRO)
     def _(m):

time: 41 us -> 40.3 us (0.983)
  the two profiles are of different devices: /device:TPU:123 before, /device:TPU:57 now
where the time goes in v3:
time: 40.3 us; the launch traced here: 40.2 us
  Pallas kernels  38.5 us (96%)
  local copies, waits for them, and re-layouts  1.67 us (4%)
    pallas_call x1, Pallas kernels, local(): pl.pallas_call(kernel, name='fields', out_shape=jax.ShapeDtypeStruct((1,...  38.5 us
    unnamed x1, local copies, waits for them, and re-layouts  1.67 us

profile of v3, /device:TPU:57, one launch (start us, length us, event | category | flops | bytes accessed | tf_op | source)
XLA Modules:
  0.0 40.2 jit_solution(13642394992693685209)
XLA Ops:
  0.0 38.5 %fields.1 = f32[1,32,16,128]{3,2,1,0:T(8,128)} custom-call(f32[1,32,16,128]{3,2,1,0:T(8,128)} %state.1, f32[1,32,16,128]{3,2,1,0:T(8,128)} %coef.1, s32[16,16,32]{2,1,0:T(8,128)} %bitcast.1, s32[8,16]{1,0:T(8,128)} %bricks_in.1, f32[8,16]{1,0:T(8,128)} %powers_in.1), custom_call_target="tpu_custom_call" | custom-call | tf_op jit(solution)/shard_map/fields/pallas_call | solution.py:438
  38.5 1.7 %copy.7 = f32[1,32,16,128]{3,2,1,0:T(8,128)} copy(f32[1,32,16,128]{3,2,1,0:T(8,128)} %fields.1) | data formatting | bytes 524288

commit v4 on v3

--- a/solution.py
+++ b/solution.py
@@ -189,15 +189,14 @@
             def _():
                 strip(kind, d).wait_send()
 
-    def pack(slot, block):
+    def pack(slot, load):
         for x in range(BX):
-            pk[slot, 0, pl.ds(H * x, H), :] = block[x, 0:H, :]
-            pk[slot, 1, pl.ds(H * x, H), :] = block[x, BY - H:BY, :]
+            pk[slot, 0, pl.ds(H * x, H), :] = load(x, 0)
+            pk[slot, 1, pl.ds(H * x, H), :] = load(x, BY - H)
 
     def send_block(block, slot, m, own, other):
         body_copy(block, m, 0).start()
         body_copy(block, m, 1).start()
-        pack(slot, block)
         start_strips(other, ALONG_Y)
         start_strips(own, ALONG_Y + ALONG_X)
         if m:
@@ -214,6 +213,7 @@
             fl[pl.ds(row_of(x + H) + H, BY), :] = pb[m, x]
 
     state_copy.wait()
+    pack(0, lambda x, y: sv[x, y:y + H, :])
     pl.semaphore_wait(barrier, count)
     send_block(sv, 0, 0, OWN0, PART0)
 
@@ -230,7 +230,7 @@
     coef_copy.wait()
     for x in range(BX):
         cv[x] = cv[x] * act[pl.ds(x, BY, stride=BX), :]
-    pack(2, cv)
+    pack(2, lambda x, y: cv[x, y:y + H, :])
     start_strips(BASE0, ALONG_Y + ALONG_X)
     body_copy(sv, 0, 2).start()
 
@@ -298,8 +298,8 @@
     relay(BASE0)
     receive_strips(OWN0, fu.at[0])
     receive_strips(BASE0, fb)
+    receive_strips(PART0, fl)
     unpack_partner(0)
-    receive_strips(PART0, fl)
 
     matrix = shift_matrix()
 
@@ -315,7 +315,8 @@
             at = pl.ds(BASE + CHUNK * i, CHUNK)
             w = fl[at, :]
             fa[at, :] = 2.0 + 0.5 * w * w
-            ff[at, :] = 6.0 * (z_next(w) - z_prev(w))
+            following, previous = z_both(w, matrix)
+            ff[at, :] = 6.0 * (following - previous)
 
     def lateral(parts, finish, skip):
         @pl.loop(0, PR // 8)
@@ -410,6 +411,7 @@
 
         @pl.when(m == 0)
         def _():
+            pack(1, lambda x, y: fu[0, pl.ds(row_of(x + H) + H + y, H), :])
             for x in range(BX):
                 nb[x] = fu[0, pl.ds(row_of(x + H) + H, BY), :]
             send_block(nb, 1, 1, OWN1, PART1)
@@ -417,8 +419,8 @@
             relay(OWN1)
             relay(PART1)
             receive_strips(OWN1, fu.at[0])
+            receive_strips(PART1, fl)
             unpack_partner(1)
-            receive_strips(PART1, fl)
 
     for x in range(BX):
         out[0, x] = fu[0, pl.ds(row_of(x + H) + H, BY), :]

time: 40.3 us -> 40.3 us (level)
  no operation moved by 1% of the time
where the time goes in v4:
time: 40.3 us; the launch traced here: 40.2 us
  Pallas kernels  38.5 us (96%)
  local copies, waits for them, and re-layouts  1.67 us (4%)
    pallas_call x1, Pallas kernels, local(): pl.pallas_call(kernel, name='fields', out_shape=jax.ShapeDtypeStruct((1,...  38.5 us
    unnamed x1, local copies, waits for them, and re-layouts  1.67 us

profile of v4, /device:TPU:57, one launch (start us, length us, event | category | flops | bytes accessed | tf_op | source)
XLA Modules:
  0.0 40.2 jit_solution(13011578952451443387)
XLA Ops:
  0.0 38.5 %fields.1 = f32[1,32,16,128]{3,2,1,0:T(8,128)} custom-call(f32[1,32,16,128]{3,2,1,0:T(8,128)} %state.1, f32[1,32,16,128]{3,2,1,0:T(8,128)} %coef.1, s32[16,16,32]{2,1,0:T(8,128)} %bitcast.1, s32[8,16]{1,0:T(8,128)} %bricks_in.1, f32[8,16]{1,0:T(8,128)} %powers_in.1), custom_call_target="tpu_custom_call" | custom-call | tf_op jit(solution)/shard_map/fields/pallas_call | solution.py:440
  38.5 1.7 %copy.7 = f32[1,32,16,128]{3,2,1,0:T(8,128)} copy(f32[1,32,16,128]{3,2,1,0:T(8,128)} %fields.1) | data formatting | bytes 524288
